TPU v7x, 256 devices: a whole 4x4x8 slice. The times are simulated.
256 devices in a mesh: wide: 32 (over z_hi, x, core), narrow: 8 (over z_lo, y).
Axes of the slice: x: 4, y: 4, z: 8 (z_hi: 4, z_lo: 2; z = z_hi * 2 + z_lo), core: 2. Of those that a mesh axis runs over, the one named last changes fastest.
Arguments:
- resid: bfloat16 [1024, 5120], P('wide'), may hold values from -6 to 6
- final_gain: float32 [5120], replicated, may hold values from 0.25 to 1.75
- unembed: bfloat16 [16384, 5120], P('narrow', 'wide'), may hold values from -12 to 12
- labels: int32 [1024, 4], replicated, may hold values from 0 to 16383
- layer_in: bfloat16 [1024, 5120], P('wide'), may hold values from -6 to 6
- gate_value: bfloat16 [1024, 13824], P('wide', 'narrow'), may hold values from -0.29882812 to 2
- down_weight: bfloat16 [13824, 5120], P('narrow', 'wide'), may hold values from -0.078125 to 0.078125
- basis_in: bfloat16 [5120, 5120], P('wide', 'narrow'), may hold values from -0.078125 to 0.078125
- basis_out: bfloat16 [13824, 13824], P('narrow', 'wide'), may hold values from -0.0546875 to 0.0546875
Outputs:
- corrected: float32 [13824, 5120], P('wide', 'narrow')
All inputs are finite; a program needn't handle non-finite values.
Results may differ from a plain program's by a relative error of at most 0.002.
The roundings to bfloat16 on the way count: a program that leaves them out, or rounds other values in their place, can miss the bound.
Values may be sent and summed in bfloat16 or wider, within the bound.
A program may use at most 128 MiB of HBM per device.

v0:
```python
import jax
import jax.numpy as jnp
from jax import lax
from jax.sharding import PartitionSpec as P

SEQ = 256
EXAMPLES = 4
EPSILON = 1e-05


def sent_to_all(value, axis):
    copies = jnp.broadcast_to(value, (lax.axis_size(axis), *value.shape))
    return lax.all_to_all(copies, axis, split_axis=0, concat_axis=0, tiled=True)


def of_everyone(value, axis):
    return sent_to_all(value, axis).sum(axis=0)


def taken_together(value, axis):
    return sent_to_all(value, axis).max(axis=0)


def contract_last(left, right):
    return lax.dot_general(
        left, right, (((1,), (1,)), ((), ())), preferred_element_type=jnp.float32
    )


def per_device(
    resid, final_gain, unembed, labels, layer_in, gate_value, down_weight, basis_in, basis_out
):
    wide_count = lax.axis_size("wide")
    wide_place = lax.axis_index("wide")
    narrow_place = lax.axis_index("narrow")
    local_tokens, width = resid.shape
    all_tokens, samples = labels.shape
    column_part = width // wide_count
    vocab_part = unembed.shape[0]
    hidden_part = down_weight.shape[0]
    grad_rows = local_tokens * samples
    resid_cols, inputs_cols = (
        lax.all_to_all(resid, "wide", split_axis=1, concat_axis=0, tiled=True),
        lax.all_to_all(layer_in, "wide", split_axis=1, concat_axis=0, tiled=True),
    )
    resid_float = resid_cols.astype(jnp.float32)
    gain_cols = lax.dynamic_slice_in_dim(final_gain, wide_place * column_part, column_part, 0)
    square_sums = of_everyone(jnp.sum(resid_float * resid_float, axis=1), "wide")
    inverse = lax.rsqrt(square_sums / width + EPSILON)
    normed = (resid_float * inverse[:, None] * gain_cols).astype(jnp.bfloat16)
    logits = lax.psum_scatter(
        contract_last(normed, unembed), "wide", scatter_dimension=0, tiled=True
    )
    largest = taken_together(jnp.max(logits, axis=1), "narrow")
    scaled = jnp.exp(logits - largest[:, None])
    totals = of_everyone(jnp.sum(scaled, axis=1), "narrow")
    probs = (scaled / totals[:, None]).astype(jnp.bfloat16)
    common = jnp.dot(
        lax.all_gather(probs, "wide", axis=0, tiled=True),
        unembed,
        preferred_element_type=jnp.float32,
    )
    shifted = labels - narrow_place * vocab_part
    inside = ((shifted >= 0) & (shifted < vocab_part)).astype(jnp.float32)
    picked = (
        jnp.take(unembed, jnp.clip(shifted, 0, vocab_part - 1), axis=0).astype(jnp.float32)
        * inside[:, :, None]
    )
    label_part = (common[:, None, :] - picked).reshape(all_tokens * samples, column_part)
    label_grads = lax.psum(label_part, "narrow")
    grads_local = lax.all_to_all(
        label_grads, "wide", split_axis=0, concat_axis=1, tiled=True
    ).reshape(local_tokens, samples, width)
    resid_local = resid.astype(jnp.float32)
    inverse_local = lax.rsqrt(jnp.mean(resid_local * resid_local, axis=1) + EPSILON)
    inner = jnp.sum(final_gain * grads_local * resid_local[:, None, :], axis=2)
    back = (
        inverse_local[:, None, None] * final_gain * grads_local
        - resid_local[:, None, :] * (inverse_local**3)[:, None, None] * inner[:, :, None] / width
    )
    back = back.astype(jnp.bfloat16).reshape(grad_rows, width)
    hidden_grads = contract_last(back, lax.all_gather(down_weight, "wide", axis=1, tiled=True))
    gated = (
        hidden_grads.reshape(local_tokens, samples, hidden_part)
        * gate_value.astype(jnp.float32)[:, None, :]
    )
    gated = gated.astype(jnp.bfloat16).reshape(grad_rows, hidden_part)
    rotated_part = jnp.dot(
        lax.all_gather(gated, "wide", axis=0, tiled=True),
        basis_out,
        preferred_element_type=jnp.float32,
    )
    rotated = lax.psum(rotated_part, "narrow").astype(jnp.bfloat16)
    inputs_part = jnp.dot(inputs_cols, basis_in, preferred_element_type=jnp.float32)
    inputs_rot = lax.psum(inputs_part, "wide").astype(jnp.bfloat16)
    rot_blocks = rotated.reshape(EXAMPLES, SEQ, samples, rotated.shape[1])
    input_blocks = inputs_rot.reshape(EXAMPLES, SEQ, inputs_rot.shape[1])
    blocks = jnp.einsum(
        "etsj,etd->esjd", rot_blocks, input_blocks, preferred_element_type=jnp.float32
    )
    return jnp.mean(blocks * blocks, axis=(0, 1))


def solution(mesh):
    in_specs = (
        P("wide", None),
        P(),
        P("narrow", "wide"),
        P(),
        P("wide", None),
        P("wide", "narrow"),
        P("narrow", "wide"),
        P("wide", "narrow"),
        P("narrow", "wide"),
    )
    out_specs = P("wide", "narrow")
    return jax.shard_map(
        per_device, mesh=mesh, in_specs=in_specs, out_specs=out_specs, check_vma=False
    )
```

profile of v0, /device:TPU:70, one launch (start us, length us, event | category | flops | bytes accessed | tf_op | source)
XLA Modules:
  0.0 968.3 jit_solution(15569779703708332936)
XLA Ops:
  8.6 26.2 %all_to_all.66 = bf16[32,32,160]{2,0,1:T(8,128)(2,1)S(1)} all-to-all(bf16[32,32,160]{2,0,1:T(8,128)(2,1)S(1)} %copy.52), channel_id=1, replica_groups=mesh['wide'=32,'narrow'=8] {'wide'}, dimensions={1} | all-to-all | bytes 655360 | tf_op jit(solution)/shard_map/all_to_all | solution.py:43
  35.8 6.7 all-to-all-start.1
  42.6 6.6 all-to-all-done.1
  54.1 119.5 %reduce-scatter.2.cloned.1.call-done = f32[32,2048]{1,0:T(8,128)} async-done(((f32[1024,2048]{1,0:T(8,128)}), f32[32,2048]{1,0:T(8,128)}) %reduce-scatter.2.cloned.1.call-update) | async-done | bytes 262160 | tf_op jit(solution)/shard_map/reduce_scatter | solution.py:51
  174.7 10.3 %all_to_all.67 = f32[8,1,32]{2,1,0:T(1,128)S(1)} all-to-all(f32[8,1,32]{2,1,0:T(1,128)S(1)} %broadcast_in_dim.41), channel_id=1, replica_groups=mesh['wide'=32,'narrow'=8] {'narrow'}, dimensions={0} | all-to-all | bytes 2048 | tf_op jit(solution)/shard_map/all_to_all | solution.py:13
  186.2 8.5 all_to_all.68
  202.4 16.9 %gather_fusion = bf16[4096,160]{1,0:T(8,128)(2,1)} fusion(bf16[2048,160]{1,0:T(8,128)(2,1)S(1)} %copy.59, s32[4096]{0:T(1024)S(1)} %broadcast_clamp_fusion), kind=kCustom, calls=%fused_computation | custom fusion | bytes 2637824 | tf_op jit(solution)/shard_map/jit(_take)/gather | solution.py:66
  219.4 34.8 %all-gather.4.cloned.1.call-done = bf16[1024,2048]{1,0:T(8,128)(2,1)} async-done(((bf16[32,2048]{1,0:T(8,128)(2,1)}), bf16[1024,2048]{1,0:T(8,128)(2,1)}) %all-gather.4.cloned.1.call-update) | async-done | bytes 4194320 | tf_op jit(solution)/shard_map/all_gather | solution.py:59
  260.3 5.3 sub.33
  265.5 7.0 multiply_subtract_fusion
  278.2 89.5 %all-reduce.4.cloned.1.call-done = f32[32,128,160]{1,2,0:T(8,128)} async-done(((f32[32,128,160]{1,2,0:T(8,128)}), f32[32,128,160]{1,2,0:T(8,128)}) %all-reduce.4.cloned.1.call-update) | async-done | bytes 2621456 | tf_op jit(solution)/shard_map/psum | solution.py:70
  367.7 9.0 all-to-all-start.4
  379.1 5.7 mul.154
  386.8 58.8 %all-to-all-done.4 = f32[32,128,160]{1,2,0:T(8,128)} async-done(((f32[32,128,160]{1,2,0:T(8,128)}), f32[32,128,160]{1,2,0:T(8,128)}, u32[]{:S(2)}, u32[]{:S(2)}) %all-to-all-start.4) | async-done | bytes 2621472 | tf_op jit(solution)/shard_map/all_to_all | solution.py:71
  455.4 5.8 reshape.127
  464.8 70.3 %all-gather.6.cloned.1.call-done = bf16[1728,5120]{0,1:T(8,128)(2,1)} async-done(((bf16[1728,160]{0,1:T(8,128)(2,1)}), bf16[1728,5120]{0,1:T(8,128)(2,1)}) %all-gather.6.cloned.1.call-update) | async-done | bytes 17694736 | tf_op jit(solution)/shard_map/all_gather | solution.py:82
  535.1 9.0 fusion.6
  546.5 36.9 %all_to_all.69 = bf16[32,32,160]{2,0,1:T(8,128)(2,1)S(1)} all-to-all(bf16[32,32,160]{2,0,1:T(8,128)(2,1)S(1)} %copy.66), channel_id=1, replica_groups=mesh['wide'=32,'narrow'=8] {'wide'}, dimensions={1} | all-to-all | bytes 655360 | tf_op jit(solution)/shard_map/all_to_all | solution.py:44
  585.4 192.2 %all-reduce.6 = bf16[1024,640]{1,0:T(8,128)(2,1)S(1)} all-reduce(f32[1024,640]{1,0:T(8,128)} %fusion.16), channel_id=1, replica_groups=mesh['wide'=32,'narrow'=8] {'wide'}, use_global_device_ids=true, to_apply=%region_11.12 | all-reduce | flops 655360 | bytes 3932160 | tf_op jit(solution)/shard_map/psum | solution.py:95
  777.7 11.7 %fusion.15 = f32[4096,432]{0,1:T(8,128)} fusion(bf16[4096,1728]{1,0:T(8,128)(2,1)} %all-gather.8.cloned.1.call-done, bf16[1728,432]{0,1:T(8,128)(2,1)S(1)} %copy-done), kind=kOutput, calls=%fused_computation.31 | convolution fusion | flops 6115295232 | bytes 22726656 | tf_op jit(solution)/shard_map/dot_general | solution.py:88
  789.4 152.2 %all-reduce.5 = bf16[4096,432]{0,1:T(8,128)(2,1)} all-reduce(f32[4096,432]{0,1:T(8,128)} %fusion.15), channel_id=1, replica_groups=mesh['wide'=32,'narrow'=8] {'narrow'}, use_global_device_ids=true, to_apply=%region_10.11 | all-reduce | flops 1769472 | bytes 10616832 | tf_op jit(solution)/shard_map/psum | solution.py:93
  941.7 6.4 copy.65
  948.1 7.0 reshape.129
  955.0 5.6 multiply_reduce_fusion
  (73 shorter events, 52.8 us)
Async XLA Ops:
  6.5 771.1 %copy-start = (bf16[1728,432]{0,1:T(8,128)(2,1)S(1)}, bf16[1728,432]{0,1:T(8,128)(2,1)}, u32[]{:S(2)}) copy-start(bf16[1728,432]{0,1:T(8,128)(2,1)} %param.17) | copy-start | bytes 4478980
  6.5 36.0 %copy-start.6 = (f32[5120]{0:T(1024)S(1)}, f32[5120]{0:T(1024)}, u32[]{:S(2)}) copy-start(f32[5120]{0:T(1024)} %param.10) | copy-start | bytes 61444
  6.5 43.0 %copy-start.2 = (bf16[2048,160]{0,1:T(8,128)(2,1)S(1)}, bf16[2048,160]{0,1:T(8,128)(2,1)}, u32[]{:S(2)}) copy-start(bf16[2048,160]{0,1:T(8,128)(2,1)} %param.11) | copy-start | bytes 1966084
  35.8 13.5 %all-to-all-start.1 = ((f32[32,1,1024]{2,1,0:T(1,128)}), f32[32,1,1024]{2,1,0:T(1,128)S(1)}, u32[]{:S(2)}, u32[]{:S(2)}) async-start(f32[32,1,1024]{2,1,0:T(1,128)} %broadcast_in_dim.40), calls=%async_computation.1 | async-start | bytes 262144 | tf_op jit(solution)/shard_map/all_to_all | solution.py:13
  42.5 131.2 %reduce-scatter.2.cloned.1.call-start = ((), (), s32[]{:S(2)}) async-start(), calls=%async_computation.7 | async-start | bytes 8650752 | tf_op jit(solution)/shard_map/reduce_scatter | solution.py:51
  54.1 143.0 %copy-start.7 = (s32[1024,4]{0,1:T(4,128)S(1)}, s32[1024,4]{0,1:T(4,128)}, u32[]{:S(2)}) copy-start(s32[1024,4]{0,1:T(4,128)} %param.12) | copy-start | bytes 49156
  54.1 200.1 %all-gather.4.cloned.1.call-start = ((), (), s32[]{:S(2)}) async-start(), calls=%async_computation.8 | async-start | bytes 4325376 | tf_op jit(solution)/shard_map/all_gather | solution.py:59
  196.5 171.2 %all-reduce.4.cloned.1.call-start = ((), (), s32[]{:S(2)}) async-start(), calls=%async_computation.9 | async-start | bytes 5242880 | tf_op jit(solution)/shard_map/psum | solution.py:70
  277.7 257.5 %all-gather.6.cloned.1.call-start = ((), (), s32[]{:S(2)}) async-start(), calls=%async_computation.10 | async-start | bytes 18923520 | tf_op jit(solution)/shard_map/all_gather | solution.py:82
  278.2 98.8 %copy-start.1 = (bf16[32,5120]{1,0:T(8,128)(2,1)S(1)}, bf16[32,5120]{1,0:T(8,128)(2,1)}, u32[]{:S(2)}) copy-start(bf16[32,5120]{1,0:T(8,128)(2,1)} %param.9) | copy-start | bytes 983044
  367.7 77.9 %all-to-all-start.4 = ((f32[32,128,160]{1,2,0:T(8,128)}), f32[32,128,160]{1,2,0:T(8,128)}, u32[]{:S(2)}, u32[]{:S(2)}) async-start(f32[32,128,160]{1,2,0:T(8,128)} %all-reduce.4.cloned.1.call-done), calls=%async_computation.5 | async-start | bytes 5242880 | tf_op jit(solution)/shard_map/all_to_all | solution.py:71
  376.7 400.9 %all-gather.8.cloned.1.call-start = ((), (), s32[]{:S(2)}) async-start(), calls=%async_computation.11 | async-start | bytes 15138816 | tf_op jit(solution)/shard_map/all_gather | solution.py:89
  379.1 5.7 copy-start.5
  464.8 80.8 %copy-start.3 = (bf16[32,5120]{1,0:T(8,128)(2,1)S(1)}, bf16[32,5120]{1,0:T(8,128)(2,1)}, u32[]{:S(2)}) copy-start(bf16[32,5120]{1,0:T(8,128)(2,1)} %param.13) | copy-start | bytes 983044
  544.2 39.2 %copy-start.4 = (bf16[160,640]{1,0:T(8,128)(2,1)S(1)}, bf16[160,640]{1,0:T(8,128)(2,1)}, u32[]{:S(2)}) copy-start(bf16[160,640]{1,0:T(8,128)(2,1)} %param.16) | copy-start | bytes 614404
Sparse Core Ops, SparseCore 0:
  54.2 119.3 reduce-scatter.1
  196.6 57.4 all-gather.3
  277.8 89.9 all-reduce.3
  370.1 164.9 all-gather.5
  545.6 118.2 all-gather.7
where the time goes:
time: 970 us; the launch traced here: 968 us
  blocking collectives  426 us (44%)
  waiting for transfers between devices  380 us (39%)
  local copies, waits for them, and re-layouts  73.3 us (8%)
  matrix products  36.3 us (4%)
  other arithmetic  22.6 us (2%)
  starting transfers between devices  16 us (2%)
  between operations  13.4 us (1%)
    psum x1, blocking collectives, per_device(): inputs_rot = lax.psum(inputs_part, 'wide').astype(jnp.bfloat16)  192 us
    psum x1, blocking collectives, per_device(): rotated = lax.psum(rotated_part, 'narrow').astype(jnp.bfloat16)  152 us
    reduce_scatter x1, waiting for transfers between devices, per_device(): lax.psum_scatter(contract_last(normed, unembed), 'wide', scatter_dimensio...  120 us
    psum x1, waiting for transfers between devices, per_device(): label_grads = lax.psum(label_part, 'narrow')  89.5 us
    all_gather x1, waiting for transfers between devices, per_device(): lax.all_gather(down_weight, 'wide', axis=1, tiled=True)  70.3 us
    all_to_all x1, waiting for transfers between devices, per_device(): lax.all_to_all(label_grads, 'wide', split_axis=0, concat_axis=1, tiled=True)  58.8 us
    all_to_all x1, blocking collectives, per_device(): lax.all_to_all(layer_in, 'wide', split_axis=1, concat_axis=0, tiled=True)  36.9 us
    all_gather x1, waiting for transfers between devices, per_device(): lax.all_gather(probs, 'wide', axis=0, tiled=True)  34.8 us
  transfers between devices with their start and end apart: 7, of which 6 were waited for; matrix products, arithmetic and copies ran while one was open for 6% of the time, Pallas kernels for 0%

commit v1 on v0

--- a/solution.py
+++ b/solution.py
@@ -79,7 +79,12 @@
         - resid_local[:, None, :] * (inverse_local**3)[:, None, None] * inner[:, :, None] / width
     )
     back = back.astype(jnp.bfloat16).reshape(grad_rows, width)
-    hidden_grads = contract_last(back, lax.all_gather(down_weight, "wide", axis=1, tiled=True))
+    hidden_grads = contract_last(
+        back,
+        jnp.concatenate(
+            lax.all_to_all(jnp.stack([down_weight] * lax.axis_size("wide")), "wide", 0, 0), axis=1
+        ),
+    )
     gated = (
         hidden_grads.reshape(local_tokens, samples, hidden_part)
         * gate_value.astype(jnp.float32)[:, None, :]

time: 970 us -> 1300 us (1.34)
  waiting for transfers between devices: 380 us -> 608 us
  blocking collectives: 426 us -> 487 us
  local copies, waits for them, and re-layouts: 73.3 us -> 96 us
    all_to_all x1, waiting for transfers between devices: 58.8 us -> 358 us  [per_device(): lax.all_to_all(jnp.stack([down_weight] * lax.axis_size('wide')), 'wide',...]
    all_gather x1 -> x0, waiting for transfers between devices: 70.3 us -> none  [per_device(): lax.all_gather(down_weight, 'wide', axis=1, tiled=True)]
    all_to_all x0 -> x1, blocking collectives: none -> 58.3 us  [per_device(): lax.all_to_all(label_grads, 'wide', split_axis=0, concat_axis=1, tiled=True)]
    all_to_all x1, blocking collectives: 36.9 us -> 18.9 us  [per_device(): lax.all_to_all(layer_in, 'wide', split_axis=1, concat_axis=0, tiled=True)]
    psum x1, blocking collectives: 192 us -> 210 us  [per_device(): inputs_rot = lax.psum(inputs_part, 'wide').astype(jnp.bfloat16)]
  transfers between devices with their start and end apart: 7 -> 6, of which waited for: 6 -> 5; matrix products, arithmetic and copies ran while one was open for 6% -> 5% of each run, Pallas kernels for 0% -> 0%
where the time goes in v1:
time: 1300 us; the launch traced here: 1290 us
  waiting for transfers between devices  608 us (47%)
  blocking collectives  487 us (37%)
  local copies, waits for them, and re-layouts  96 us (7%)
  matrix products  36.4 us (3%)
  starting transfers between devices  25.3 us (2%)
  other arithmetic  22.2 us (2%)
  between operations  13.4 us (1%)
    all_to_all x1, waiting for transfers between devices, per_device(): lax.all_to_all(jnp.stack([down_weight] * lax.axis_size('wide')), 'wide',...  358 us
    psum x1, blocking collectives, per_device(): inputs_rot = lax.psum(inputs_part, 'wide').astype(jnp.bfloat16)  210 us
    psum x1, blocking collectives, per_device(): rotated = lax.psum(rotated_part, 'narrow').astype(jnp.bfloat16)  155 us
    reduce_scatter x1, waiting for transfers between devices, per_device(): lax.psum_scatter(contract_last(normed, unembed), 'wide', scatter_dimensio...  120 us
    psum x1, waiting for transfers between devices, per_device(): label_grads = lax.psum(label_part, 'narrow')  90 us
    all_to_all x1, blocking collectives, per_device(): lax.all_to_all(label_grads, 'wide', split_axis=0, concat_axis=1, tiled=True)  58.3 us
    all_gather x1, waiting for transfers between devices, per_device(): lax.all_gather(probs, 'wide', axis=0, tiled=True)  34.7 us
    all_to_all x1, blocking collectives, per_device(): lax.all_to_all(resid, 'wide', split_axis=1, concat_axis=0, tiled=True)  26.2 us
  transfers between devices with their start and end apart: 6, of which 5 were waited for; matrix products, arithmetic and copies ran while one was open for 5% of the time, Pallas kernels for 0%

profile of v1, /device:TPU:70, one launch (start us, length us, event | category | flops | bytes accessed | tf_op | source)
XLA Modules:
  0.0 1288.3 jit_solution(7564494500762712051)
XLA Ops:
  8.6 26.2 %all_to_all.71 = bf16[32,32,160]{2,0,1:T(8,128)(2,1)S(1)} all-to-all(bf16[32,32,160]{2,0,1:T(8,128)(2,1)S(1)} %copy.55), channel_id=1, replica_groups=mesh['wide'=32,'narrow'=8] {'wide'}, dimensions={1} | all-to-all | bytes 655360 | tf_op jit(solution)/shard_map/all_to_all | solution.py:43
  35.8 6.7 all-to-all-start.1
  43.3 6.0 all-to-all-done.1
  54.1 119.8 %reduce-scatter.2.cloned.1.call-done = f32[32,2048]{1,0:T(8,128)} async-done(((f32[1024,2048]{1,0:T(8,128)}), f32[32,2048]{1,0:T(8,128)}) %reduce-scatter.2.cloned.1.call-update) | async-done | bytes 262160 | tf_op jit(solution)/shard_map/reduce_scatter | solution.py:51
  175.0 10.2 all_to_all.72
  186.4 8.5 all_to_all.73
  202.6 16.9 %gather_fusion = bf16[4096,160]{1,0:T(8,128)(2,1)} fusion(bf16[2048,160]{1,0:T(8,128)(2,1)S(1)} %copy.62, s32[4096]{0:T(1024)S(1)} %broadcast_clamp_fusion), kind=kCustom, calls=%fused_computation | custom fusion | bytes 2637824 | tf_op jit(solution)/shard_map/jit(_take)/gather | solution.py:66
  219.6 34.7 %all-gather.3.cloned.1.call-done = bf16[1024,2048]{1,0:T(8,128)(2,1)} async-done(((bf16[32,2048]{1,0:T(8,128)(2,1)}), bf16[1024,2048]{1,0:T(8,128)(2,1)}) %all-gather.3.cloned.1.call-update) | async-done | bytes 4194320 | tf_op jit(solution)/shard_map/all_gather | solution.py:59
  265.7 7.0 multiply_subtract_fusion
  277.8 90.0 %all-reduce.4.cloned.1.call-done = f32[32,128,160]{1,2,0:T(8,128)} async-done(((f32[32,128,160]{1,2,0:T(8,128)}), f32[32,128,160]{1,2,0:T(8,128)}) %all-reduce.4.cloned.1.call-update) | async-done | bytes 2621456 | tf_op jit(solution)/shard_map/psum | solution.py:70
  367.8 58.3 %all_to_all.74 = f32[32,128,160]{1,2,0:T(8,128)} all-to-all(f32[32,128,160]{1,2,0:T(8,128)} %all-reduce.4.cloned.1.call-done), channel_id=1, replica_groups=mesh['wide'=32,'narrow'=8] {'wide'}, dimensions={0} | all-to-all | bytes 5242880 | tf_op jit(solution)/shard_map/all_to_all | solution.py:71
  426.1 6.5 stack.2
  432.6 18.5 %all-to-all-start.5 = ((bf16[32,1728,160]{1,2,0:T(8,128)(2,1)}), bf16[32,1728,160]{1,2,0:T(8,128)(2,1)}, u32[]{:S(2)}, u32[]{:S(2)}) async-start(bf16[32,1728,160]{1,2,0:T(8,128)(2,1)} %stack.2), calls=%async_computation.6 | async-start | bytes 36700160 | tf_op jit(solution)/shard_map/all_to_all | solution.py:85
  461.5 5.6 mul.139
  469.4 5.7 mul.155
  495.2 357.9 %all-to-all-done.5 = bf16[32,1728,160]{1,2,0:T(8,128)(2,1)} async-done(((bf16[32,1728,160]{1,2,0:T(8,128)(2,1)}), bf16[32,1728,160]{1,2,0:T(8,128)(2,1)}, u32[]{:S(2)}, u32[]{:S(2)}) %all-to-all-start.5) | async-done | bytes 17694752 | tf_op jit(solution)/shard_map/all_to_all | solution.py:85
  853.0 9.1 fusion.5
  864.5 18.9 %all_to_all.75 = bf16[32,32,160]{2,0,1:T(8,128)(2,1)S(1)} all-to-all(bf16[32,32,160]{2,0,1:T(8,128)(2,1)S(1)} %copy.70), channel_id=1, replica_groups=mesh['wide'=32,'narrow'=8] {'wide'}, dimensions={1} | all-to-all | bytes 655360 | tf_op jit(solution)/shard_map/all_to_all | solution.py:44
  885.4 210.0 %all-reduce.6 = bf16[1024,640]{1,0:T(8,128)(2,1)S(1)} all-reduce(f32[1024,640]{1,0:T(8,128)} %fusion.13), channel_id=1, replica_groups=mesh['wide'=32,'narrow'=8] {'wide'}, use_global_device_ids=true, to_apply=%region_11.12 | all-reduce | flops 655360 | bytes 3932160 | tf_op jit(solution)/shard_map/psum | solution.py:100
  1095.4 11.7 fusion.12
  1107.1 154.5 %all-reduce.5 = bf16[4096,432]{0,1:T(8,128)(2,1)} all-reduce(f32[4096,432]{0,1:T(8,128)} %fusion.12), channel_id=1, replica_groups=mesh['wide'=32,'narrow'=8] {'narrow'}, use_global_device_ids=true, to_apply=%region_10.11 | all-reduce | flops 1769472 | bytes 10616832 | tf_op jit(solution)/shard_map/psum | solution.py:98
  1261.6 6.4 copy.69
  1268.0 7.0 reshape.141
  1275.0 5.6 multiply_reduce_fusion
  (81 shorter events, 73.3 us)
Async XLA Ops:
  6.5 1088.9 %copy-start = (bf16[1728,432]{0,1:T(8,128)(2,1)S(1)}, bf16[1728,432]{0,1:T(8,128)(2,1)}, u32[]{:S(2)}) copy-start(bf16[1728,432]{0,1:T(8,128)(2,1)} %param.17) | copy-start | bytes 4478980
  6.5 43.0 %copy-start.4 = (bf16[2048,160]{0,1:T(8,128)(2,1)S(1)}, bf16[2048,160]{0,1:T(8,128)(2,1)}, u32[]{:S(2)}) copy-start(bf16[2048,160]{0,1:T(8,128)(2,1)} %param.11) | copy-start | bytes 1966084
  35.8 13.5 %all-to-all-start.1 = ((f32[32,1,1024]{2,1,0:T(1,128)}), f32[32,1,1024]{2,1,0:T(1,128)S(1)}, u32[]{:S(2)}, u32[]{:S(2)}) async-start(f32[32,1,1024]{2,1,0:T(1,128)} %broadcast_in_dim.40), calls=%async_computation.1 | async-start | bytes 262144 | tf_op jit(solution)/shard_map/all_to_all | solution.py:13
  42.5 131.5 %reduce-scatter.2.cloned.1.call-start = ((), (), s32[]{:S(2)}) async-start(), calls=%async_computation.8 | async-start | bytes 8650752 | tf_op jit(solution)/shard_map/reduce_scatter | solution.py:51
  54.1 143.2 %copy-start.10 = (s32[1024,4]{0,1:T(4,128)S(1)}, s32[1024,4]{0,1:T(4,128)}, u32[]{:S(2)}) copy-start(s32[1024,4]{0,1:T(4,128)} %param.12) | copy-start | bytes 49156
  54.1 200.2 %all-gather.3.cloned.1.call-start = ((), (), s32[]{:S(2)}) async-start(), calls=%async_computation.9 | async-start | bytes 4325376 | tf_op jit(solution)/shard_map/all_gather | solution.py:59
  196.7 171.1 %all-reduce.4.cloned.1.call-start = ((), (), s32[]{:S(2)}) async-start(), calls=%async_computation.10 | async-start | bytes 5242880 | tf_op jit(solution)/shard_map/psum | solution.py:70
  277.8 148.3 %copy-start.5 = (bf16[1728,160]{0,1:T(8,128)(2,1)S(1)}, bf16[1728,160]{0,1:T(8,128)(2,1)}, u32[]{:S(2)}) copy-start(bf16[1728,160]{0,1:T(8,128)(2,1)} %param.15) | copy-start | bytes 1658884
  432.6 18.5 %copy-start.9 = (f32[5120]{0:T(1024)S(1)}, f32[5120]{0:T(1024)}, u32[]{:S(2)}) copy-start(f32[5120]{0:T(1024)} %param.10) | copy-start | bytes 61444
  432.6 18.6 %copy-start.3 = (bf16[32,5120]{1,0:T(8,128)(2,1)S(1)}, bf16[32,5120]{1,0:T(8,128)(2,1)}, u32[]{:S(2)}) copy-start(bf16[32,5120]{1,0:T(8,128)(2,1)} %param.9) | copy-start | bytes 983044
  432.6 420.5 %all-to-all-start.5 = ((bf16[32,1728,160]{1,2,0:T(8,128)(2,1)}), bf16[32,1728,160]{1,2,0:T(8,128)(2,1)}, u32[]{:S(2)}, u32[]{:S(2)}) async-start(bf16[32,1728,160]{1,2,0:T(8,128)(2,1)} %stack.2), calls=%async_computation.6 | async-start | bytes 36700160 | tf_op jit(solution)/shard_map/all_to_all | solution.py:85
  451.1 644.3 %all-gather.5.cloned.1.call-start = ((), (), s32[]{:S(2)}) async-start(), calls=%async_computation.11 | async-start | bytes 15138816 | tf_op jit(solution)/shard_map/all_gather | solution.py:94
  469.4 5.7 copy-start.8
  480.2 4.7 copy-start.1
  480.2 5.9 copy-start.2
  853.0 10.5 copy-start.6
  862.1 21.2 %copy-start.7 = (bf16[160,640]{1,0:T(8,128)(2,1)S(1)}, bf16[160,640]{1,0:T(8,128)(2,1)}, u32[]{:S(2)}) copy-start(bf16[160,640]{1,0:T(8,128)(2,1)} %param.16) | copy-start | bytes 614404
Sparse Core Ops, SparseCore 0:
  54.2 119.6 reduce-scatter.1
  196.8 57.4 all-gather.2
  277.9 89.8 all-reduce.3
  863.6 138.0 all-gather.4
